TPU v7x, 32 devices: a whole 2x2x4 slice. The times are simulated.
32 devices in a mesh: groups: 2 (over y), ctx: 4 (over z), tp: 2 (over x), kv: 2 (over core).
Axes of the slice: x: 2, y: 2, z: 4, core: 2. Of those that a mesh axis runs over, the one named last changes fastest.
Arguments:
- queries: bfloat16 [2048, 8192], P(('groups', 'ctx'), ('tp', 'kv')), parts along dimension 0, may hold values from -8 to 8
- key_matrix: bfloat16 [2048, 1024], P(('groups', 'ctx'), 'tp'), parts along dimension 0, may hold values from -8 to 8
- value_matrix: bfloat16 [2048, 1024], P(('groups', 'ctx'), 'tp'), parts along dimension 0, may hold values from -6 to 6
- out_grad: bfloat16 [2048, 8192], P(('groups', 'ctx'), ('tp', 'kv')), parts along dimension 0, may hold values from -6 to 6
- segments: int32 [2048], P(('groups', 'ctx')), parts along dimension 0, may hold values from 0 to 15, never falling along the last dimension, each value on 1 to 512 neighbouring positions
Outputs:
- query_grad: bfloat16 [2048, 8192], P(('groups', 'ctx'), ('tp', 'kv')), parts along dimension 0
- key_gradient: bfloat16 [2048, 1024], P(('groups', 'ctx'), 'tp'), parts along dimension 0
- value_gradient: bfloat16 [2048, 1024], P(('groups', 'ctx'), 'tp'), parts along dimension 0
There are 2 independent parts, one for each index of `groups`. A program takes and returns all parts, laid end to end along the dimension named above; each array names one. Nothing has to cross between parts.
Inputs may be any that keep to these rules, and one draw needn't show every extreme that they name: `segments`: document numbers never fall along the sequence; each of the 16 documents has 1 or more positions and one document holds exactly half of the 1024 positions.
All inputs are finite; a program needn't handle non-finite values.
Results may differ from a plain program's by a relative error of at most 0.011.
Values may be sent and summed in bfloat16 or wider, within the bound.
A program may use at most 64 MiB of HBM per device.

v0:
```python
import functools
import jax
import jax.numpy as jnp
from jax import lax
from jax.experimental import pallas as pl
from jax.experimental.pallas import tpu as pltpu
from jax.sharding import PartitionSpec as P

QUERY_HEADS = 64
KEY_VALUE_HEADS = 8
HEAD_SIZE = 128
HALF = 128
CHUNK = 32
LOG2E = 1.4426950408889634
NEG = -1e30
MESH = pl.DeviceIdType.MESH
NT = (((1,), (1,)), ((), ()))


def kernel(
    n, reach, rows, per_kv, kv_count, shared,
    q_hbm, k_hbm, v_hbm, g_hbm, seg_hbm,
    dqv, fin, other,
    qv, gv, sv, dpv, peaks, pv, dsv, win, segwin, segcol, bias, kt, acc, sendb, ret, pfin,
    load_sem, own_sem, seg_send, seg_recv, send_sem, recv_sem, back_send, back_recv,
    pair_send, pair_recv,
):
    rank = lax.axis_index("ctx")
    kv = lax.axis_index("kv")
    up = lax.rem(rank + 1, n)
    down = lax.rem(rank + n - 1, n)
    mate = 1 - kv
    scale = HEAD_SIZE ** -0.5
    width = reach * rows + HALF
    halves = rows // HALF
    first = 0 if shared else kv * kv_count

    def cols(base, g):
        if shared:
            return pl.ds(g * HEAD_SIZE, HEAD_SIZE)
        return pl.ds(pl.multiple_of((base + g) * HEAD_SIZE, HEAD_SIZE), HEAD_SIZE)

    def slot(d):
        return pl.ds((reach - d) * rows, rows)

    loads = [
        pltpu.make_async_copy(q_hbm, qv, load_sem.at[0]),
        pltpu.make_async_copy(g_hbm, gv, load_sem.at[1]),
    ]
    seg_load = pltpu.make_async_copy(seg_hbm, segwin.at[0], load_sem.at[2])
    owns = []
    for g in range(kv_count):
        for t, ref in ((0, k_hbm), (1, v_hbm)):
            owns.append(
                pltpu.make_async_copy(
                    ref.at[:, cols(first, g)], win.at[t, g, slot(0)], own_sem.at[t, g]
                )
            )

    def forward(t, g, d):
        ref = k_hbm if t == 0 else v_hbm
        src = ref.at[:, cols(first, g)] if d == 0 else win.at[t, g, slot(d)]
        return pltpu.make_async_remote_copy(
            src_ref=src,
            dst_ref=win.at[t, g, slot(d + 1)],
            send_sem=send_sem.at[t, g, d],
            recv_sem=recv_sem.at[t, g, d + 1],
            device_id={"ctx": up},
            device_id_type=MESH,
        )

    def forward_seg(d):
        return pltpu.make_async_remote_copy(
            src_ref=seg_hbm if d == 0 else segwin.at[d],
            dst_ref=segwin.at[d + 1],
            send_sem=seg_send.at[d],
            recv_sem=seg_recv.at[d + 1],
            device_id={"ctx": up},
            device_id_type=MESH,
        )

    pieces = [(t, r) for t in range(2) for r in range(halves)]

    def some(r):
        return pl.ds(r * HALF, HALF)

    def back(g, d, t, r):
        return pltpu.make_async_remote_copy(
            src_ref=sendb.at[g, d - 1, t, some(r)],
            dst_ref=ret.at[g, d - 1, t, some(r)],
            send_sem=back_send.at[g, d - 1, t, r],
            recv_sem=back_recv.at[g, d - 1, t, r],
            device_id={"ctx": down},
            device_id_type=MESH,
        )

    def owed(g, d, t, r):
        return acc[g, t, pl.ds((reach - d) * rows + r * HALF, HALF), :]

    def to_mate(g, t, r):
        return pltpu.make_async_remote_copy(
            src_ref=fin.at[g, t, some(r)],
            dst_ref=pfin.at[g, t, some(r)],
            send_sem=pair_send.at[g, t, r],
            recv_sem=pair_recv.at[g, t, r],
            device_id={"kv": mate},
            device_id_type=MESH,
        )

    has_up = rank < n - 1

    for copy in [seg_load] + owns + loads:
        copy.start()

    barrier = pltpu.get_barrier_semaphore()
    pl.semaphore_signal(barrier, inc=1, device_id={"kv": mate}, device_id_type=MESH)

    @pl.when(has_up)
    def _():
        pl.semaphore_signal(barrier, inc=1, device_id={"ctx": up}, device_id_type=MESH)

    @pl.when(rank > 0)
    def _():
        pl.semaphore_signal(barrier, inc=1, device_id={"ctx": down}, device_id_type=MESH)

    expected = 1 + jnp.where(has_up, 1, 0) + jnp.where(rank > 0, 1, 0)
    pl.semaphore_wait(barrier, expected)

    @pl.when(has_up)
    def _():
        forward_seg(0).start()
        forward(0, 0, 0).start()
        forward(1, 0, 0).start()

    for d in range(1, reach + 1):
        @pl.when(rank < d)
        def _(d=d):
            for g in range(kv_count):
                for t in range(2):
                    win[t, g, slot(d), :] = jnp.zeros((rows, HEAD_SIZE), jnp.bfloat16)
            segwin[d] = jnp.full((1, rows), -1, jnp.int32)

    acc[...] = jnp.zeros_like(acc)

    def pass_on_seg():
        for d in range(1, reach + 1):
            @pl.when(rank >= d)
            def _(d=d):
                forward_seg(d - 1).wait_recv()

            if d < reach:
                @pl.when((rank >= d) & has_up)
                def _(d=d):
                    forward_seg(d).start()

    def pass_on(g, kinds):
        for d in range(1, reach):
            for t in kinds:
                @pl.when(rank >= d)
                def _(d=d, t=t):
                    forward(t, g, d - 1).wait_recv()

                @pl.when((rank >= d) & has_up)
                def _(d=d, t=t):
                    forward(t, g, d).start()

    def last_slot(g):
        @pl.when(rank >= reach)
        def _():
            for t in range(2):
                forward(t, g, reach - 1).wait_recv()

    def send_own(g):
        @pl.when(has_up)
        def _():
            for t in range(2):
                forward(t, g, 0).start()

    def make_bias():
        for d in range(reach + 1):
            row = segwin[d].astype(jnp.float32)
            segcol[slot(d), :] = jnp.broadcast_to(row, (HALF, rows)).T
        key_at = lax.broadcasted_iota(jnp.int32, (width, HALF), 0)
        query_at = lax.broadcasted_iota(jnp.int32, (width, HALF), 1)
        causal = key_at <= query_at + reach * rows
        for h in range(halves):
            seg_q = segwin[0, :, h * HALF:(h + 1) * HALF].astype(jnp.float32)
            same = segcol[h * HALF:h * HALF + width, :] == seg_q
            bias[h] = jnp.where(same & causal, 0.0, NEG)

    def spot(g, h, p):
        c0 = pl.multiple_of((g * per_kv + 2 * p) * HEAD_SIZE, HEAD_SIZE)
        c1 = pl.multiple_of((g * per_kv + 2 * p + 1) * HEAD_SIZE, HEAD_SIZE)
        part = slice(h * HALF, (h + 1) * HALF)
        return part, pl.ds(c0, HEAD_SIZE), pl.ds(c1, HEAD_SIZE)

    def pair(ref, g, h, p):
        part, one, two = spot(g, h, p)
        return jnp.concatenate([ref[part, one], ref[part, two]], axis=0)

    def span(h):
        return slice(h * HALF, h * HALF + width)

    def products(g, h, p):
        s = lax.dot_general(
            win[0, g, span(h), :], pair(qv, g, h, p), NT, preferred_element_type=jnp.float32
        )
        b = bias[h]
        s = s + jnp.concatenate([b, b], axis=1)
        sv[h] = s
        peaks[h] = jnp.max(s, axis=0, keepdims=True)
        dpv[h] = lax.dot_general(
            win[1, g, span(h), :], pair(gv, g, h, p), NT, preferred_element_type=jnp.float32
        )

    def softmax(h):
        peak = peaks[h]
        total = jnp.zeros((8, 2 * HALF), jnp.float32)
        weighted = jnp.zeros((8, 2 * HALF), jnp.float32)
        for c in range(0, width, CHUNK):
            rows_c = slice(c, c + CHUNK)
            e = jnp.exp2((sv[h, rows_c, :] - peak) * (scale * LOG2E))
            sv[h, rows_c, :] = e
            total = total + jnp.sum(e.reshape(-1, 8, 2 * HALF), axis=0)
            weighted = weighted + jnp.sum(
                (e * dpv[h, rows_c, :]).reshape(-1, 8, 2 * HALF), axis=0
            )
        inv = 1.0 / jnp.sum(total, axis=0, keepdims=True)
        delta = jnp.sum(weighted, axis=0, keepdims=True) * inv
        for c in range(0, width, CHUNK):
            rows_c = slice(c, c + CHUNK)
            pn = sv[h, rows_c, :] * inv
            dsv[h, rows_c, :] = (pn * (dpv[h, rows_c, :] - delta)).astype(jnp.bfloat16)
            pv[h, rows_c, :] = pn.astype(jnp.bfloat16)

    def grads(g, h, p):
        part, one, two = spot(g, h, p)
        ds = dsv[h]
        dqt = jnp.dot(kt[g, :, span(h)], ds, preferred_element_type=jnp.float32)
        dq = (dqt * scale).T.astype(jnp.bfloat16)
        dqv[part, one] = dq[:HALF]
        dqv[part, two] = dq[HALF:]
        acc[g, 0, span(h), :] += jnp.dot(
            ds, pair(qv, g, h, p), preferred_element_type=jnp.float32
        )
        acc[g, 1, span(h), :] += jnp.dot(
            pv[h], pair(gv, g, h, p), preferred_element_type=jnp.float32
        )

    pairs = per_kv // 2
    last_half = halves - 1

    def begin_units(g):
        dsv[last_half] = jnp.zeros((width, 2 * HALF), jnp.bfloat16)
        pv[last_half] = jnp.zeros((width, 2 * HALF), jnp.bfloat16)
        products(g, 0, 0)

    def units(g, begin, end):
        def body(p, carry):
            for h in range(halves):
                if h < last_half:
                    products(g, h + 1, p)
                else:
                    products(g, 0, jnp.minimum(p + 1, pairs - 1))
                softmax(h)
                if h > 0:
                    grads(g, h - 1, p)
                else:
                    grads(g, last_half, jnp.maximum(p - 1, 0))
            return carry

        lax.fori_loop(begin, end, body, 0)

    def end_units(g):
        grads(g, last_half, pairs - 1)

    def send_first(g):
        for d in range(reach, 0, -1):
            @pl.when((rank >= d) if d == reach else jnp.logical_not(has_up))
            def _(d=d):
                for t, r in pieces:
                    sendb[g, d - 1, t, some(r), :] = owed(g, d, t, r).astype(jnp.bfloat16)
                    back(g, d, t, r).start()

    def send_rest(g):
        for d in range(reach - 1, 0, -1):
            @pl.when(has_up & (rank >= d))
            def _(d=d):
                for t, r in pieces:
                    back(g, d + 1, t, r).wait_recv()
                    sendb[g, d - 1, t, some(r), :] = (
                        owed(g, d, t, r) + ret[g, d, t, some(r), :].astype(jnp.float32)
                    ).astype(jnp.bfloat16)
                    back(g, d, t, r).start()

    def finish(g):
        for t, r in pieces:
            @pl.when(has_up)
            def _(t=t, r=r):
                back(g, 1, t, r).wait_recv()
                acc[g, t, pl.ds(reach * rows + r * HALF, HALF), :] += (
                    ret[g, 0, t, some(r), :].astype(jnp.float32)
                )

            factor = scale if t == 0 else 1.0
            fin[g, t, some(r), :] = (owed(g, 0, t, r) * factor).astype(jnp.bfloat16)
            to_mate(g, t, r).start()

    pass_on_seg()
    seg_load.wait()
    make_bias()
    pass_on(0, (0, 1))
    for copy in loads + owns:
        copy.wait()
    early, middle, late = pairs // 4, pairs // 2, pairs * 3 // 4
    for g in range(kv_count):
        if g + 1 < kv_count:
            send_own(g + 1)
        last_slot(g)
        kt[g] = win[0, g].T
        begin_units(g)
        if g + 1 < kv_count:
            units(g, 0, early)
            pass_on(g + 1, (0,))
            units(g, early, middle)
            pass_on(g + 1, (1,))
            if g > 0:
                send_rest(g - 1)
            units(g, middle, pairs)
        elif g > 0:
            units(g, 0, late)
            send_rest(g - 1)
            units(g, late, pairs)
        else:
            units(g, 0, pairs)
        end_units(g)
        send_first(g)
    send_rest(kv_count - 1)
    for g in range(kv_count):
        finish(g)

    for g in range(kv_count):
        for t in range(2):
            for r in range(halves):
                to_mate(g, t, r).wait()
            if shared:
                other[g, t] = (
                    fin[g, t].astype(jnp.float32) + pfin[g, t].astype(jnp.float32)
                ).astype(jnp.bfloat16)
            else:
                other[g, t] = pfin[g, t]
    for d in range(reach):
        @pl.when(has_up & (rank >= d))
        def _(d=d):
            forward_seg(d).wait_send()
            for g in range(kv_count):
                for t in range(2):
                    forward(t, g, d).wait_send()
    for d in range(1, reach + 1):
        @pl.when(rank >= d)
        def _(d=d):
            for g in range(kv_count):
                for t, r in pieces:
                    back(g, d, t, r).wait_send()


def place(kv_count, shared, dqv, fin, other, dq_hbm, dk_hbm, dv_hbm, sem):
    kv = lax.axis_index("kv")
    copies = [pltpu.make_async_copy(dqv, dq_hbm, sem.at[0])]
    parts = [(other, 0)] if shared else [(fin, kv * kv_count), (other, (1 - kv) * kv_count)]
    for source, base in parts:
        for g in range(kv_count):
            start = g * HEAD_SIZE
            if not shared:
                start = pl.multiple_of((base + g) * HEAD_SIZE, HEAD_SIZE)
            for t, ref in ((0, dk_hbm), (1, dv_hbm)):
                copies.append(
                    pltpu.make_async_copy(
                        source.at[g, t], ref.at[:, pl.ds(start, HEAD_SIZE)], sem.at[len(copies)]
                    )
                )
    for copy in copies:
        copy.start()
    for copy in copies:
        copy.wait()


def shards(queries, key_matrix, value_matrix, out_grad, segments):
    n = lax.axis_size("ctx")
    rows = queries.shape[0]
    head_count = queries.shape[1] // HEAD_SIZE
    group_width = QUERY_HEADS // KEY_VALUE_HEADS
    kv_count = max(head_count // group_width, 1)
    per_kv = head_count // kv_count
    kv_here = key_matrix.shape[1] // HEAD_SIZE
    shared = kv_here < kv_count * lax.axis_size("kv")
    reach = n // 2
    window = (reach + 1) * rows
    width = reach * rows + HALF
    halves = rows // HALF
    bf16, f32 = jnp.bfloat16, jnp.float32
    dma = pltpu.SemaphoreType.DMA
    anywhere = pl.BlockSpec(memory_space=pltpu.HBM)
    inner = pltpu.VMEM
    dqv, fin, other = pl.pallas_call(
        functools.partial(kernel, n, reach, rows, per_kv, kv_count, shared),
        out_shape=(
            inner(queries.shape, bf16),
            inner((kv_count, 2, rows, HEAD_SIZE), bf16),
            inner((kv_count, 2, rows, HEAD_SIZE), bf16),
        ),
        in_specs=[anywhere] * 5,
        out_specs=(pl.BlockSpec(memory_space=pltpu.VMEM),) * 3,
        scratch_shapes=[
            pltpu.VMEM(queries.shape, bf16),
            pltpu.VMEM(queries.shape, bf16),
            pltpu.VMEM((halves, width, 2 * HALF), f32),
            pltpu.VMEM((halves, width, 2 * HALF), f32),
            pltpu.VMEM((halves, 1, 2 * HALF), f32),
            pltpu.VMEM((halves, width, 2 * HALF), bf16),
            pltpu.VMEM((halves, width, 2 * HALF), bf16),
            pltpu.VMEM((2, kv_count, window, HEAD_SIZE), bf16),
            pltpu.VMEM((reach + 1, 1, rows), jnp.int32),
            pltpu.VMEM((window, HALF), f32),
            pltpu.VMEM((halves, width, HALF), f32),
            pltpu.VMEM((kv_count, HEAD_SIZE, window), bf16),
            pltpu.VMEM((kv_count, 2, window, HEAD_SIZE), f32),
            pltpu.VMEM((kv_count, reach, 2, rows, HEAD_SIZE), bf16),
            pltpu.VMEM((kv_count, reach, 2, rows, HEAD_SIZE), bf16),
            pltpu.VMEM((kv_count, 2, rows, HEAD_SIZE), bf16),
            dma((3,)),
            dma((2, kv_count)),
            dma((reach + 1,)),
            dma((reach + 1,)),
            dma((2, kv_count, reach + 1)),
            dma((2, kv_count, reach + 1)),
            dma((kv_count, reach, 2, halves)),
            dma((kv_count, reach, 2, halves)),
            dma((kv_count, 2, halves)),
            dma((kv_count, 2, halves)),
        ],
        compiler_params=pltpu.CompilerParams(
            collective_id=0, has_side_effects=True, vmem_limit_bytes=56 * 1024 * 1024
        ),
    )(queries, key_matrix, value_matrix, out_grad, segments.reshape(1, rows))
    return pl.pallas_call(
        functools.partial(place, kv_count, shared),
        out_shape=(
            jax.ShapeDtypeStruct(queries.shape, bf16),
            jax.ShapeDtypeStruct(key_matrix.shape, bf16),
            jax.ShapeDtypeStruct(value_matrix.shape, bf16),
        ),
        in_specs=[pl.BlockSpec(memory_space=pltpu.VMEM)] * 3,
        out_specs=(anywhere,) * 3,
        scratch_shapes=[dma((1 + 4 * kv_count,))],
        compiler_params=pltpu.CompilerParams(vmem_limit_bytes=4 * 1024 * 1024),
    )(dqv, fin, other)


def solution(mesh):
    return jax.shard_map(
        shards,
        mesh=mesh,
        in_specs=(
            P(("groups", "ctx"), ("tp", "kv")),
            P(("groups", "ctx"), "tp"),
            P(("groups", "ctx"), "tp"),
            P(("groups", "ctx"), ("tp", "kv")),
            P(("groups", "ctx")),
        ),
        out_specs=(
            P(("groups", "ctx"), ("tp", "kv")),
            P(("groups", "ctx"), "tp"),
            P(("groups", "ctx"), "tp"),
        ),
        check_vma=False,
    )
```

profile of v0, /device:TPU:0, one launch (start us, length us, event | category | flops | bytes accessed | tf_op | source)
XLA Modules:
  0.0 36.3 jit_solution(13721364882528985506)
XLA Ops:
  0.6 34.4 %shard_map.76 = (bf16[256,2048]{1,0:T(8,128)(2,1)S(1)}, bf16[2,2,256,128]{3,2,1,0:T(8,128)(2,1)S(1)}, bf16[2,2,256,128]{3,2,1,0:T(8,128)(2,1)S(1)}) custom-call(bf16[256,2048]{1,0:T(8,128)(2,1)} %q_hbm.1, bf16[256,512]{1,0:T(8,128)(2,1)} %k_hbm.1, bf16[256,512]{1,0:T(8,128)(2,1)} %v_hbm.1, bf16[256,2048]{1,0:T(8,128)(2,1)} %g_hbm.1, s32[1,256]{1,0:T(1,128)} %bitcast.1), custom_call_target="tpu_custom_call" | custom-call | tf_op jit(solution)/shard_map/pallas_call | solution.py:405
  35.1 1.2 %shard_map.77 = (bf16[256,2048]{1,0:T(8,128)(2,1)}, bf16[256,512]{1,0:T(8,128)(2,1)}, bf16[256,512]{1,0:T(8,128)(2,1)}) custom-call(bf16[256,2048]{1,0:T(8,128)(2,1)S(1)} %get-tuple-element.6.dqv, bf16[2,2,256,128]{3,2,1,0:T(8,128)(2,1)S(1)} %get-tuple-element.7.fin, bf16[2,2,256,128]{3,2,1,0:T(8,128)(2,1)S(1)} %get-tuple-element.8.other), custom_call_target="tpu_custom_call" | custom-call | tf_op jit(solution)/shard_map/pallas_call | solution.py:446
where the time goes:
time: 36.4 us; the launch traced here: 36.3 us
  Pallas kernels  35.6 us (98%)
  between operations  0.64 us (2%)
    pallas_call x1, Pallas kernels, shards(): pl.pallas_call(functools.partial(kernel, n, reach, rows, per_kv, kv_count...  34.4 us
    pallas_call x1, Pallas kernels, shards(): pl.pallas_call(functools.partial(place, kv_count, shared), out_shape=(jax...  1.2 us

commit v1 on v0

v1 whole, which is shorter than its diff:
```python
import functools
import jax
import jax.numpy as jnp
from jax import lax
from jax.experimental import pallas as pl
from jax.experimental.pallas import tpu as pltpu
from jax.sharding import PartitionSpec as P

QUERY_HEADS = 64
KEY_VALUE_HEADS = 8
HEAD_SIZE = 128
HALF = 128
CHUNK = 32
LOG2E = 1.4426950408889634
NEG = -1e30
MESH = pl.DeviceIdType.MESH
NT = (((1,), (1,)), ((), ()))


def kernel(
    n, reach, rows, per_kv, kv_count, shared,
    q_hbm, k_hbm, v_hbm, g_hbm, seg_hbm,
    dqv, fin, other,
    qv, gv, ev, dpv, stats, fac, deltas, pv, dsv, win, segwin, bias, kt, acc, sendb, ret, pfin,
    seg_sem, load_sem, own_sem, seg_send, seg_recv, send_sem, recv_sem, back_send, back_recv,
    pair_send, pair_recv,
):
    rank = lax.axis_index("ctx")
    kv = lax.axis_index("kv")
    up = lax.rem(rank + 1, n)
    down = lax.rem(rank + n - 1, n)
    mate = 1 - kv
    scale = HEAD_SIZE ** -0.5
    width = reach * rows + HALF
    halves = rows // HALF
    pairs = per_kv // 2
    first = 0 if shared else kv * kv_count

    def cols(base, g):
        if shared:
            return pl.ds(g * HEAD_SIZE, HEAD_SIZE)
        return pl.ds(pl.multiple_of((base + g) * HEAD_SIZE, HEAD_SIZE), HEAD_SIZE)

    def slot(d):
        return pl.ds((reach - d) * rows, rows)

    seg_load = pltpu.make_async_copy(seg_hbm, segwin.at[0], seg_sem.at[0])

    def own(t, g):
        ref = k_hbm if t == 0 else v_hbm
        return pltpu.make_async_copy(
            ref.at[:, cols(first, g)], win.at[t, g, slot(0)], own_sem.at[t, g]
        )

    def load(t, head):
        ref, to = ((q_hbm, qv), (g_hbm, gv))[t]
        return pltpu.make_async_copy(
            ref.at[:, pl.ds(head * HEAD_SIZE, HEAD_SIZE)], to.at[head], load_sem.at[t, head]
        )

    def group_loads(g):
        heads = range(g * per_kv, (g + 1) * per_kv)
        return [own(t, g) for t in range(2)] + [load(t, i) for i in heads for t in range(2)]

    def forward(t, g, d):
        ref = k_hbm if t == 0 else v_hbm
        src = ref.at[:, cols(first, g)] if d == 0 else win.at[t, g, slot(d)]
        return pltpu.make_async_remote_copy(
            src_ref=src,
            dst_ref=win.at[t, g, slot(d + 1)],
            send_sem=send_sem.at[t, g, d],
            recv_sem=recv_sem.at[t, g, d + 1],
            device_id={"ctx": up},
            device_id_type=MESH,
        )

    def forward_seg(d):
        return pltpu.make_async_remote_copy(
            src_ref=seg_hbm if d == 0 else segwin.at[d],
            dst_ref=segwin.at[d + 1],
            send_sem=seg_send.at[d],
            recv_sem=seg_recv.at[d + 1],
            device_id={"ctx": up},
            device_id_type=MESH,
        )

    def pieces(kinds):
        return [(t, r) for t in kinds for r in range(halves)]

    def some(r):
        return pl.ds(r * HALF, HALF)

    def back(g, d, t, r):
        return pltpu.make_async_remote_copy(
            src_ref=sendb.at[g, d - 1, t, some(r)],
            dst_ref=ret.at[g, d - 1, t, some(r)],
            send_sem=back_send.at[g, d - 1, t, r],
            recv_sem=back_recv.at[g, d - 1, t, r],
            device_id={"ctx": down},
            device_id_type=MESH,
        )

    def owed(g, d, t, r):
        return acc[g, t, pl.ds((reach - d) * rows + r * HALF, HALF), :]

    def to_mate(g, t, r):
        return pltpu.make_async_remote_copy(
            src_ref=fin.at[g, t, some(r)],
            dst_ref=pfin.at[g, t, some(r)],
            send_sem=pair_send.at[g, t, r],
            recv_sem=pair_recv.at[g, t, r],
            device_id={"kv": mate},
            device_id_type=MESH,
        )

    has_up = rank < n - 1

    seg_load.start()
    for g in range(kv_count):
        for copy in group_loads(g):
            copy.start()

    barrier = pltpu.get_barrier_semaphore()
    pl.semaphore_signal(barrier, inc=1, device_id={"kv": mate}, device_id_type=MESH)

    @pl.when(has_up)
    def _():
        pl.semaphore_signal(barrier, inc=1, device_id={"ctx": up}, device_id_type=MESH)

    @pl.when(rank > 0)
    def _():
        pl.semaphore_signal(barrier, inc=1, device_id={"ctx": down}, device_id_type=MESH)

    expected = 1 + jnp.where(has_up, 1, 0) + jnp.where(rank > 0, 1, 0)
    pl.semaphore_wait(barrier, expected)

    @pl.when(has_up)
    def _():
        forward_seg(0).start()
        forward(0, 0, 0).start()
        forward(1, 0, 0).start()

    units = pairs * halves

    def pass_on_seg():
        for d in range(1, reach + 1):
            @pl.when(rank >= d)
            def _(d=d):
                forward_seg(d - 1).wait_recv()

            if d < reach:
                @pl.when((rank >= d) & has_up)
                def _(d=d):
                    forward_seg(d).start()

    def receive(g, d, t):
        @pl.when(rank >= d)
        def _():
            forward(t, g, d - 1).wait_recv()

        if d < reach:
            @pl.when((rank >= d) & has_up)
            def _():
                forward(t, g, d).start()

    def send_own(g):
        @pl.when(has_up)
        def _():
            for t in range(2):
                forward(t, g, 0).start()

    def part(d, h):
        start = (reach - d) * rows - h * HALF
        return max(start, 0), min(start + rows, width)

    def make_bias(d):
        column = jnp.broadcast_to(segwin[d].astype(jnp.float32), (HALF, rows)).T
        for h in range(halves):
            lo, hi = part(d, h)
            begin = lo + h * HALF - (reach - d) * rows
            seg_q = segwin[0, :, h * HALF:(h + 1) * HALF].astype(jnp.float32)
            keep = column[begin:begin + hi - lo] == seg_q
            if d == 0:
                key_at = lax.broadcasted_iota(jnp.int32, (hi - lo, HALF), 0)
                query_at = lax.broadcasted_iota(jnp.int32, (hi - lo, HALF), 1)
                keep = keep & (key_at + begin <= query_at + h * HALF)
            bias[h, lo:hi, :] = jnp.where(keep, 0.0, NEG)

    def pair(ref, g, h, p):
        head = g * per_kv + 2 * p
        return ref[head:head + 2, h * HALF:(h + 1) * HALF, :].reshape(2 * HALF, HEAD_SIZE)

    def stack(ref, g, h):
        return ref[g * per_kv:(g + 1) * per_kv, h * HALF:(h + 1) * HALF, :].reshape(
            per_kv * HALF, HEAD_SIZE
        )

    def products(g, d, p, h):
        lo, hi = part(d, h)
        span = slice(lo + h * HALF, hi + h * HALF)
        s = lax.dot_general(
            win[0, g, span, :], pair(qv, g, h, p), NT, preferred_element_type=jnp.float32
        )
        b = bias[h, lo:hi, :]
        s = s + jnp.concatenate([b, b], axis=1)
        ev[g, p, h, lo:hi, :] = s
        u = p * halves + h
        stats[g, d, 0, u:u + 1, :] = jnp.max(s, axis=0, keepdims=True)
        dpv[g, p, h, lo:hi, :] = lax.dot_general(
            win[1, g, span, :], pair(gv, g, h, p), NT, preferred_element_type=jnp.float32
        )

    def exponentials(g, d, p, h):
        lo, hi = part(d, h)
        u = p * halves + h
        peak = stats[g, d, 0, u:u + 1, :]
        total = jnp.zeros((8, 2 * HALF), jnp.float32)
        weighted = jnp.zeros((8, 2 * HALF), jnp.float32)
        for c in range(lo, hi, CHUNK):
            at = slice(c, c + CHUNK)
            e = jnp.exp2((ev[g, p, h, at, :] - peak) * (scale * LOG2E))
            ev[g, p, h, at, :] = e
            total = total + jnp.sum(e.reshape(-1, 8, 2 * HALF), axis=0)
            weighted = weighted + jnp.sum(
                (e * dpv[g, p, h, at, :]).reshape(-1, 8, 2 * HALF), axis=0
            )
        stats[g, d, 1, u:u + 1, :] = jnp.sum(total, axis=0, keepdims=True)
        stats[g, d, 2, u:u + 1, :] = jnp.sum(weighted, axis=0, keepdims=True)

    def look(g, d):
        @pl.when(rank >= d)
        def _():
            todo = [(p, h) for p in range(pairs) for h in range(halves)]
            products(g, d, *todo[0])
            for i, at in enumerate(todo):
                if i + 1 < len(todo):
                    products(g, d, *todo[i + 1])
                exponentials(g, d, *at)

    def combine(g):
        peak = stats[g, 0, 0]
        for d in range(1, reach + 1):
            peak = jnp.maximum(peak, stats[g, d, 0])
        total = jnp.zeros((units, 2 * HALF), jnp.float32)
        weighted = jnp.zeros((units, 2 * HALF), jnp.float32)
        for d in range(reach + 1):
            f = jnp.exp2((stats[g, d, 0] - peak) * (scale * LOG2E))
            total = total + f * stats[g, d, 1]
            weighted = weighted + f * stats[g, d, 2]
        inv = 1.0 / total
        for d in range(reach + 1):
            f = jnp.exp2((stats[g, d, 0] - peak) * (scale * LOG2E))
            fac[d] = f * inv
        deltas[...] = weighted * inv

    def scores(g, d, h):
        lo, hi = part(d, h)
        for p in range(pairs):
            u = p * halves + h
            f = fac[d, u:u + 1, :]
            delta = deltas[u:u + 1, :]
            there = slice(p * 2 * HALF, (p + 1) * 2 * HALF)
            for c in range(lo, hi, CHUNK):
                at = slice(c, c + CHUNK)
                pn = ev[g, p, h, at, :] * f
                dsv[h, at, there] = (pn * (dpv[g, p, h, at, :] - delta)).astype(jnp.bfloat16)
                pv[h, at, there] = pn.astype(jnp.bfloat16)

    def gradients(g, d, h, add):
        lo, hi = part(d, h)
        span = slice(lo + h * HALF, hi + h * HALF)
        for t, low, ref in ((0, dsv, qv), (1, pv, gv)):
            out = jnp.dot(
                low[h, lo:hi, :], stack(ref, g, h), preferred_element_type=jnp.float32
            )
            if add:
                acc[g, t, span, :] += out
            else:
                acc[g, t, span, :] = out

    def settle(g, d):
        @pl.when(rank >= d)
        def _():
            order = list(range(halves)) if d > 0 else list(range(halves - 1, -1, -1))
            kt[g, :, slot(d)] = win[0, g, slot(d), :].T
            for h in order:
                scores(g, d, h)
            for i, h in enumerate(order):
                gradients(g, d, h, i > 0)

    def query_gradients(g):
        for h in range(halves):
            dqt = jnp.dot(
                kt[g, :, h * HALF:h * HALF + width], dsv[h], preferred_element_type=jnp.float32
            )
            dq = (dqt * scale).T.astype(jnp.bfloat16)
            for i in range(per_kv):
                at = (g * per_kv + i) * HEAD_SIZE
                dqv[h * HALF:(h + 1) * HALF, at:at + HEAD_SIZE] = dq[i * HALF:(i + 1) * HALF]

    def send_first(g, d):
        @pl.when((rank >= d) if d == reach else ((rank >= d) & jnp.logical_not(has_up)))
        def _():
            for t, r in pieces((0, 1)):
                sendb[g, d - 1, t, some(r), :] = owed(g, d, t, r).astype(jnp.bfloat16)
                back(g, d, t, r).start()

    def send_rest(g, kinds):
        for d in range(reach - 1, 0, -1):
            @pl.when(has_up & (rank >= d))
            def _(d=d):
                for t, r in pieces(kinds):
                    back(g, d + 1, t, r).wait_recv()
                    sendb[g, d - 1, t, some(r), :] = (
                        owed(g, d, t, r) + ret[g, d, t, some(r), :].astype(jnp.float32)
                    ).astype(jnp.bfloat16)
                    back(g, d, t, r).start()

    def finish(g):
        for t, r in pieces((0, 1)):
            @pl.when(has_up)
            def _(t=t, r=r):
                back(g, 1, t, r).wait_recv()
                acc[g, t, pl.ds(reach * rows + r * HALF, HALF), :] += (
                    ret[g, 0, t, some(r), :].astype(jnp.float32)
                )

            factor = scale if t == 0 else 1.0
            fin[g, t, some(r), :] = (owed(g, 0, t, r) * factor).astype(jnp.bfloat16)
            to_mate(g, t, r).start()

    for d in range(1, reach + 1):
        @pl.when(rank < d)
        def _(d=d):
            for g in range(kv_count):
                kt[g, :, slot(d)] = jnp.zeros((HEAD_SIZE, rows), jnp.bfloat16)
                stats[g, d, 0] = jnp.full((units, 2 * HALF), NEG, jnp.float32)
                stats[g, d, 1] = jnp.zeros((units, 2 * HALF), jnp.float32)
                stats[g, d, 2] = jnp.zeros((units, 2 * HALF), jnp.float32)
            for h in range(halves):
                lo, hi = part(d, h)
                dsv[h, lo:hi, :] = jnp.zeros((hi - lo, pairs * 2 * HALF), jnp.bfloat16)

    last = kv_count - 1
    seg_load.wait()
    make_bias(0)
    for copy in group_loads(0):
        copy.wait()
    look(0, 0)
    pass_on_seg()
    for d in range(1, reach):
        for t in range(2):
            receive(0, d, t)
    if last > 0:
        send_own(1)
    for d in range(1, reach + 1):
        @pl.when(rank >= d)
        def _(d=d):
            make_bias(d)
    for d in range(1, reach):
        look(0, d)
    for g in range(kv_count):
        if g + 1 < kv_count:
            for copy in group_loads(g + 1):
                copy.wait()
            look(g + 1, 0)
        for t in range(2):
            receive(g, reach, t)
        look(g, reach)
        combine(g)
        for d in range(reach, 0, -1):
            settle(g, d)
            send_first(g, d)
        if g + 1 < kv_count:
            for d in range(1, reach):
                for t in range(2):
                    receive(g + 1, d, t)
            if g + 2 < kv_count:
                send_own(g + 2)
        settle(g, 0)
        query_gradients(g)
        if g + 1 < kv_count:
            for d in range(1, reach):
                look(g + 1, d)
        send_rest(g, (0, 1))
    for g in range(kv_count):
        finish(g)

    for g in range(kv_count):
        for t in range(2):
            for r in range(halves):
                to_mate(g, t, r).wait()
            if shared:
                other[g, t] = (
                    fin[g, t].astype(jnp.float32) + pfin[g, t].astype(jnp.float32)
                ).astype(jnp.bfloat16)
            else:
                other[g, t] = pfin[g, t]
    for d in range(reach):
        @pl.when(has_up & (rank >= d))
        def _(d=d):
            forward_seg(d).wait_send()
            for g in range(kv_count):
                for t in range(2):
                    forward(t, g, d).wait_send()
    for d in range(1, reach + 1):
        @pl.when(rank >= d)
        def _(d=d):
            for g in range(kv_count):
                for t, r in pieces((0, 1)):
                    back(g, d, t, r).wait_send()


def place(kv_count, shared, dqv, fin, other, dq_hbm, dk_hbm, dv_hbm, sem):
    kv = lax.axis_index("kv")
    copies = [pltpu.make_async_copy(dqv, dq_hbm, sem.at[0])]
    parts = [(other, 0)] if shared else [(fin, kv * kv_count), (other, (1 - kv) * kv_count)]
    for source, base in parts:
        for g in range(kv_count):
            start = g * HEAD_SIZE
            if not shared:
                start = pl.multiple_of((base + g) * HEAD_SIZE, HEAD_SIZE)
            for t, ref in ((0, dk_hbm), (1, dv_hbm)):
                copies.append(
                    pltpu.make_async_copy(
                        source.at[g, t], ref.at[:, pl.ds(start, HEAD_SIZE)], sem.at[len(copies)]
                    )
                )
    for copy in copies:
        copy.start()
    for copy in copies:
        copy.wait()


def shards(queries, key_matrix, value_matrix, out_grad, segments):
    n = lax.axis_size("ctx")
    rows = queries.shape[0]
    head_count = queries.shape[1] // HEAD_SIZE
    group_width = QUERY_HEADS // KEY_VALUE_HEADS
    kv_count = max(head_count // group_width, 1)
    per_kv = head_count // kv_count
    kv_here = key_matrix.shape[1] // HEAD_SIZE
    shared = kv_here < kv_count * lax.axis_size("kv")
    reach = n // 2
    window = (reach + 1) * rows
    width = reach * rows + HALF
    halves = rows // HALF
    pairs = per_kv // 2
    bf16, f32 = jnp.bfloat16, jnp.float32
    dma = pltpu.SemaphoreType.DMA
    anywhere = pl.BlockSpec(memory_space=pltpu.HBM)
    inner = pltpu.VMEM
    dqv, fin, other = pl.pallas_call(
        functools.partial(kernel, n, reach, rows, per_kv, kv_count, shared),
        out_shape=(
            inner(queries.shape, bf16),
            inner((kv_count, 2, rows, HEAD_SIZE), bf16),
            inner((kv_count, 2, rows, HEAD_SIZE), bf16),
        ),
        in_specs=[anywhere] * 5,
        out_specs=(pl.BlockSpec(memory_space=pltpu.VMEM),) * 3,
        scratch_shapes=[
            pltpu.VMEM((head_count, rows, HEAD_SIZE), bf16),
            pltpu.VMEM((head_count, rows, HEAD_SIZE), bf16),
            pltpu.VMEM((kv_count, pairs, halves, width, 2 * HALF), f32),
            pltpu.VMEM((kv_count, pairs, halves, width, 2 * HALF), f32),
            pltpu.VMEM((kv_count, reach + 1, 3, pairs * halves, 2 * HALF), f32),
            pltpu.VMEM((reach + 1, pairs * halves, 2 * HALF), f32),
            pltpu.VMEM((pairs * halves, 2 * HALF), f32),
            pltpu.VMEM((halves, width, pairs * 2 * HALF), bf16),
            pltpu.VMEM((halves, width, pairs * 2 * HALF), bf16),
            pltpu.VMEM((2, kv_count, window, HEAD_SIZE), bf16),
            pltpu.VMEM((reach + 1, 1, rows), jnp.int32),
            pltpu.VMEM((halves, width, HALF), f32),
            pltpu.VMEM((kv_count, HEAD_SIZE, window), bf16),
            pltpu.VMEM((kv_count, 2, window, HEAD_SIZE), f32),
            pltpu.VMEM((kv_count, reach, 2, rows, HEAD_SIZE), bf16),
            pltpu.VMEM((kv_count, reach, 2, rows, HEAD_SIZE), bf16),
            pltpu.VMEM((kv_count, 2, rows, HEAD_SIZE), bf16),
            dma((1,)),
            dma((2, head_count)),
            dma((2, kv_count)),
            dma((reach + 1,)),
            dma((reach + 1,)),
            dma((2, kv_count, reach + 1)),
            dma((2, kv_count, reach + 1)),
            dma((kv_count, reach, 2, halves)),
            dma((kv_count, reach, 2, halves)),
            dma((kv_count, 2, halves)),
            dma((kv_count, 2, halves)),
        ],
        compiler_params=pltpu.CompilerParams(
            collective_id=0, has_side_effects=True, vmem_limit_bytes=56 * 1024 * 1024
        ),
    )(queries, key_matrix, value_matrix, out_grad, segments.reshape(1, rows))
    return pl.pallas_call(
        functools.partial(place, kv_count, shared),
        out_shape=(
            jax.ShapeDtypeStruct(queries.shape, bf16),
            jax.ShapeDtypeStruct(key_matrix.shape, bf16),
            jax.ShapeDtypeStruct(value_matrix.shape, bf16),
        ),
        in_specs=[pl.BlockSpec(memory_space=pltpu.VMEM)] * 3,
        out_specs=(anywhere,) * 3,
        scratch_shapes=[dma((1 + 4 * kv_count,))],
        compiler_params=pltpu.CompilerParams(vmem_limit_bytes=4 * 1024 * 1024),
    )(dqv, fin, other)


def solution(mesh):
    return jax.shard_map(
        shards,
        mesh=mesh,
        in_specs=(
            P(("groups", "ctx"), ("tp", "kv")),
            P(("groups", "ctx"), "tp"),
            P(("groups", "ctx"), "tp"),
            P(("groups", "ctx"), ("tp", "kv")),
            P(("groups", "ctx")),
        ),
        out_specs=(
            P(("groups", "ctx"), ("tp", "kv")),
            P(("groups", "ctx"), "tp"),
            P(("groups", "ctx"), "tp"),
        ),
        check_vma=False,
    )
```

time: 36.4 us -> 31.9 us (0.88)
  Pallas kernels: 35.6 us -> 31.1 us
    pallas_call x1, Pallas kernels: 34.4 us -> 29.9 us  [shards(): pl.pallas_call(functools.partial(kernel, n, reach, rows, per_kv, kv_count...]
where the time goes in v1:
time: 31.9 us; the launch traced here: 31.7 us
  Pallas kernels  31.1 us (97%)
  between operations  0.64 us (2%)
    pallas_call x1, Pallas kernels, shards(): pl.pallas_call(functools.partial(kernel, n, reach, rows, per_kv, kv_count...  29.9 us
    pallas_call x1, Pallas kernels, shards(): pl.pallas_call(functools.partial(place, kv_count, shared), out_shape=(jax...  1.2 us

profile of v1, /device:TPU:0, one launch (start us, length us, event | category | flops | bytes accessed | tf_op | source)
XLA Modules:
  0.0 31.7 jit_solution(163820714667370258)
XLA Ops:
  0.6 29.9 %shard_map.76 = (bf16[256,2048]{1,0:T(8,128)(2,1)S(1)}, bf16[2,2,256,128]{3,2,1,0:T(8,128)(2,1)S(1)}, bf16[2,2,256,128]{3,2,1,0:T(8,128)(2,1)S(1)}) custom-call(bf16[256,2048]{1,0:T(8,128)(2,1)} %q_hbm.1, bf16[256,512]{1,0:T(8,128)(2,1)} %k_hbm.1, bf16[256,512]{1,0:T(8,128)(2,1)} %v_hbm.1, bf16[256,2048]{1,0:T(8,128)(2,1)} %g_hbm.1, s32[1,256]{1,0:T(1,128)} %bitcast.1), custom_call_target="tpu_custom_call" | custom-call | tf_op jit(solution)/shard_map/pallas_call | solution.py:453
  30.5 1.2 %shard_map.77 = (bf16[256,2048]{1,0:T(8,128)(2,1)}, bf16[256,512]{1,0:T(8,128)(2,1)}, bf16[256,512]{1,0:T(8,128)(2,1)}) custom-call(bf16[256,2048]{1,0:T(8,128)(2,1)S(1)} %get-tuple-element.6.dqv, bf16[2,2,256,128]{3,2,1,0:T(8,128)(2,1)S(1)} %get-tuple-element.7.fin, bf16[2,2,256,128]{3,2,1,0:T(8,128)(2,1)S(1)} %get-tuple-element.8.other), custom_call_target="tpu_custom_call" | custom-call | tf_op jit(solution)/shard_map/pallas_call | solution.py:496

commit v2 on v1

--- a/solution.py
+++ b/solution.py
@@ -58,9 +58,8 @@
             ref.at[:, pl.ds(head * HEAD_SIZE, HEAD_SIZE)], to.at[head], load_sem.at[t, head]
         )
 
-    def group_loads(g):
-        heads = range(g * per_kv, (g + 1) * per_kv)
-        return [own(t, g) for t in range(2)] + [load(t, i) for i in heads for t in range(2)]
+    def group_loads(g, t):
+        return [own(t, g)] + [load(t, i) for i in range(g * per_kv, (g + 1) * per_kv)]
 
     def forward(t, g, d):
         ref = k_hbm if t == 0 else v_hbm
@@ -117,8 +116,9 @@
 
     seg_load.start()
     for g in range(kv_count):
-        for copy in group_loads(g):
-            copy.start()
+        for t in range(2):
+            for copy in group_loads(g, t):
+                copy.start()
 
     barrier = pltpu.get_barrier_semaphore()
     pl.semaphore_signal(barrier, inc=1, device_id={"kv": mate}, device_id_type=MESH)
@@ -138,20 +138,18 @@
     def _():
         forward_seg(0).start()
         forward(0, 0, 0).start()
-        forward(1, 0, 0).start()
 
     units = pairs * halves
 
-    def pass_on_seg():
-        for d in range(1, reach + 1):
-            @pl.when(rank >= d)
-            def _(d=d):
-                forward_seg(d - 1).wait_recv()
-
-            if d < reach:
-                @pl.when((rank >= d) & has_up)
-                def _(d=d):
-                    forward_seg(d).start()
+    def receive_seg(d):
+        @pl.when(rank >= d)
+        def _():
+            forward_seg(d - 1).wait_recv()
+
+        if d < reach:
+            @pl.when((rank >= d) & has_up)
+            def _():
+                forward_seg(d).start()
 
     def receive(g, d, t):
         @pl.when(rank >= d)
@@ -163,11 +161,10 @@
             def _():
                 forward(t, g, d).start()
 
-    def send_own(g):
+    def send_own(g, t):
         @pl.when(has_up)
         def _():
-            for t in range(2):
-                forward(t, g, 0).start()
+            forward(t, g, 0).start()
 
     def part(d, h):
         start = (reach - d) * rows - h * HALF
@@ -186,6 +183,11 @@
                 keep = keep & (key_at + begin <= query_at + h * HALF)
             bias[h, lo:hi, :] = jnp.where(keep, 0.0, NEG)
 
+    def biased(d):
+        @pl.when(rank >= d)
+        def _():
+            make_bias(d)
+
     def pair(ref, g, h, p):
         head = g * per_kv + 2 * p
         return ref[head:head + 2, h * HALF:(h + 1) * HALF, :].reshape(2 * HALF, HEAD_SIZE)
@@ -195,7 +197,7 @@
             per_kv * HALF, HEAD_SIZE
         )
 
-    def products(g, d, p, h):
+    def key_products(g, d, p, h):
         lo, hi = part(d, h)
         span = slice(lo + h * HALF, hi + h * HALF)
         s = lax.dot_general(
@@ -206,89 +208,102 @@
         ev[g, p, h, lo:hi, :] = s
         u = p * halves + h
         stats[g, d, 0, u:u + 1, :] = jnp.max(s, axis=0, keepdims=True)
-        dpv[g, p, h, lo:hi, :] = lax.dot_general(
-            win[1, g, span, :], pair(gv, g, h, p), NT, preferred_element_type=jnp.float32
-        )
 
     def exponentials(g, d, p, h):
         lo, hi = part(d, h)
         u = p * halves + h
         peak = stats[g, d, 0, u:u + 1, :]
         total = jnp.zeros((8, 2 * HALF), jnp.float32)
-        weighted = jnp.zeros((8, 2 * HALF), jnp.float32)
         for c in range(lo, hi, CHUNK):
             at = slice(c, c + CHUNK)
             e = jnp.exp2((ev[g, p, h, at, :] - peak) * (scale * LOG2E))
             ev[g, p, h, at, :] = e
             total = total + jnp.sum(e.reshape(-1, 8, 2 * HALF), axis=0)
-            weighted = weighted + jnp.sum(
-                (e * dpv[g, p, h, at, :]).reshape(-1, 8, 2 * HALF), axis=0
-            )
         stats[g, d, 1, u:u + 1, :] = jnp.sum(total, axis=0, keepdims=True)
-        stats[g, d, 2, u:u + 1, :] = jnp.sum(weighted, axis=0, keepdims=True)
-
-    def look(g, d):
-        @pl.when(rank >= d)
-        def _():
-            todo = [(p, h) for p in range(pairs) for h in range(halves)]
-            products(g, d, *todo[0])
+
+    def value_products(g, d, p, h):
+        lo, hi = part(d, h)
+        span = slice(lo + h * HALF, hi + h * HALF)
+        u = p * halves + h
+        dp = lax.dot_general(
+            win[1, g, span, :], pair(gv, g, h, p), NT, preferred_element_type=jnp.float32
+        )
+        dpv[g, p, h, lo:hi, :] = dp
+        stats[g, d, 2, u:u + 1, :] = jnp.sum(ev[g, p, h, lo:hi, :] * dp, axis=0, keepdims=True)
+
+    todo = [(p, h) for p in range(pairs) for h in range(halves)]
+
+    def look_keys(g, d):
+        @pl.when(rank >= d)
+        def _():
+            key_products(g, d, *todo[0])
             for i, at in enumerate(todo):
                 if i + 1 < len(todo):
-                    products(g, d, *todo[i + 1])
+                    key_products(g, d, *todo[i + 1])
                 exponentials(g, d, *at)
 
-    def combine(g):
+    def look_values(g, d):
+        @pl.when(rank >= d)
+        def _():
+            for at in todo:
+                value_products(g, d, *at)
+
+    def combine_keys(g):
         peak = stats[g, 0, 0]
         for d in range(1, reach + 1):
             peak = jnp.maximum(peak, stats[g, d, 0])
         total = jnp.zeros((units, 2 * HALF), jnp.float32)
+        for d in range(reach + 1):
+            f = jnp.exp2((stats[g, d, 0] - peak) * (scale * LOG2E))
+            fac[g, d] = f
+            total = total + f * stats[g, d, 1]
+        inv = 1.0 / total
+        for d in range(reach + 1):
+            fac[g, d] = fac[g, d] * inv
+
+    def combine_values(g):
         weighted = jnp.zeros((units, 2 * HALF), jnp.float32)
         for d in range(reach + 1):
-            f = jnp.exp2((stats[g, d, 0] - peak) * (scale * LOG2E))
-            total = total + f * stats[g, d, 1]
-            weighted = weighted + f * stats[g, d, 2]
-        inv = 1.0 / total
+            weighted = weighted + fac[g, d] * stats[g, d, 2]
+        deltas[g] = weighted
+
+    def settle(g, d, t):
+        @pl.when(rank >= d)
+        def _():
+            order = list(range(halves)) if d > 0 else list(range(halves - 1, -1, -1))
+            for i, h in enumerate(order):
+                lo, hi = part(d, h)
+                for p in range(pairs):
+                    u = p * halves + h
+                    f = fac[g, d, u:u + 1, :]
+                    there = slice(p * 2 * HALF, (p + 1) * 2 * HALF)
+                    for c in range(lo, hi, CHUNK):
+                        at = slice(c, c + CHUNK)
+                        pn = ev[g, p, h, at, :] * f
+                        if t == 0:
+                            delta = deltas[g, u:u + 1, :]
+                            dsv[h, at, there] = (
+                                pn * (dpv[g, p, h, at, :] - delta)
+                            ).astype(jnp.bfloat16)
+                        else:
+                            pv[h, at, there] = pn.astype(jnp.bfloat16)
+            for i, h in enumerate(order):
+                lo, hi = part(d, h)
+                span = slice(lo + h * HALF, hi + h * HALF)
+                low, ref = ((dsv, qv), (pv, gv))[t]
+                out = jnp.dot(
+                    low[h, lo:hi, :], stack(ref, g, h), preferred_element_type=jnp.float32
+                )
+                if i > 0:
+                    acc[g, t, span, :] += out
+                else:
+                    acc[g, t, span, :] = out
+
+    def query_gradients(g):
         for d in range(reach + 1):
-            f = jnp.exp2((stats[g, d, 0] - peak) * (scale * LOG2E))
-            fac[d] = f * inv
-        deltas[...] = weighted * inv
-
-    def scores(g, d, h):
-        lo, hi = part(d, h)
-        for p in range(pairs):
-            u = p * halves + h
-            f = fac[d, u:u + 1, :]
-            delta = deltas[u:u + 1, :]
-            there = slice(p * 2 * HALF, (p + 1) * 2 * HALF)
-            for c in range(lo, hi, CHUNK):
-                at = slice(c, c + CHUNK)
-                pn = ev[g, p, h, at, :] * f
-                dsv[h, at, there] = (pn * (dpv[g, p, h, at, :] - delta)).astype(jnp.bfloat16)
-                pv[h, at, there] = pn.astype(jnp.bfloat16)
-
-    def gradients(g, d, h, add):
-        lo, hi = part(d, h)
-        span = slice(lo + h * HALF, hi + h * HALF)
-        for t, low, ref in ((0, dsv, qv), (1, pv, gv)):
-            out = jnp.dot(
-                low[h, lo:hi, :], stack(ref, g, h), preferred_element_type=jnp.float32
-            )
-            if add:
-                acc[g, t, span, :] += out
-            else:
-                acc[g, t, span, :] = out
-
-    def settle(g, d):
-        @pl.when(rank >= d)
-        def _():
-            order = list(range(halves)) if d > 0 else list(range(halves - 1, -1, -1))
-            kt[g, :, slot(d)] = win[0, g, slot(d), :].T
-            for h in order:
-                scores(g, d, h)
-            for i, h in enumerate(order):
-                gradients(g, d, h, i > 0)
-
-    def query_gradients(g):
+            @pl.when(rank >= d)
+            def _(d=d):
+                kt[g, :, slot(d)] = win[0, g, slot(d), :].T
         for h in range(halves):
             dqt = jnp.dot(
                 kt[g, :, h * HALF:h * HALF + width], dsv[h], preferred_element_type=jnp.float32
@@ -298,10 +313,10 @@
                 at = (g * per_kv + i) * HEAD_SIZE
                 dqv[h * HALF:(h + 1) * HALF, at:at + HEAD_SIZE] = dq[i * HALF:(i + 1) * HALF]
 
-    def send_first(g, d):
+    def send_first(g, d, kinds):
         @pl.when((rank >= d) if d == reach else ((rank >= d) & jnp.logical_not(has_up)))
         def _():
-            for t, r in pieces((0, 1)):
+            for t, r in pieces(kinds):
                 sendb[g, d - 1, t, some(r), :] = owed(g, d, t, r).astype(jnp.bfloat16)
                 back(g, d, t, r).start()
 
@@ -316,8 +331,8 @@
                     ).astype(jnp.bfloat16)
                     back(g, d, t, r).start()
 
-    def finish(g):
-        for t, r in pieces((0, 1)):
+    def finish(g, kinds):
+        for t, r in pieces(kinds):
             @pl.when(has_up)
             def _(t=t, r=r):
                 back(g, 1, t, r).wait_recv()
@@ -344,47 +359,68 @@
     last = kv_count - 1
     seg_load.wait()
     make_bias(0)
-    for copy in group_loads(0):
+    for copy in group_loads(0, 0):
         copy.wait()
-    look(0, 0)
-    pass_on_seg()
+    look_keys(0, 0)
     for d in range(1, reach):
-        for t in range(2):
-            receive(0, d, t)
-    if last > 0:
-        send_own(1)
-    for d in range(1, reach + 1):
-        @pl.when(rank >= d)
-        def _(d=d):
-            make_bias(d)
+        receive_seg(d)
     for d in range(1, reach):
-        look(0, d)
+        receive(0, d, 0)
+    send_own(0, 1)
+    for d in range(1, reach):
+        biased(d)
+        look_keys(0, d)
+    for copy in group_loads(0, 1):
+        copy.wait()
+    look_values(0, 0)
+    receive_seg(reach)
+    biased(reach)
     for g in range(kv_count):
-        if g + 1 < kv_count:
-            for copy in group_loads(g + 1):
+        more = g < last
+        receive(g, reach, 0)
+        look_keys(g, reach)
+        combine_keys(g)
+        for d in range(reach, 0, -1):
+            settle(g, d, 1)
+            send_first(g, d, (1,))
+        for d in range(1, reach):
+            receive(g, d, 1)
+        if more:
+            send_own(g + 1, 0)
+        for d in range(1, reach):
+            look_values(g, d)
+        if g > 0:
+            send_rest(g - 1, (0,))
+            query_gradients(g - 1)
+        if more:
+            for copy in group_loads(g + 1, 0):
                 copy.wait()
-            look(g + 1, 0)
-        for t in range(2):
-            receive(g, reach, t)
-        look(g, reach)
-        combine(g)
+            look_keys(g + 1, 0)
+        receive(g, reach, 1)
+        look_values(g, reach)
+        combine_values(g)
         for d in range(reach, 0, -1):
-            settle(g, d)
-            send_first(g, d)
-        if g + 1 < kv_count:
+            settle(g, d, 0)
+            send_first(g, d, (0,))
+        if more:
             for d in range(1, reach):
-                for t in range(2):
-                    receive(g + 1, d, t)
-            if g + 2 < kv_count:
-                send_own(g + 2)
-        settle(g, 0)
-        query_gradients(g)
-        if g + 1 < kv_count:
+                receive(g + 1, d, 0)
+            send_own(g + 1, 1)
             for d in range(1, reach):
-                look(g + 1, d)
-        send_rest(g, (0, 1))
-    for g in range(kv_count):
-        finish(g)
+                look_keys(g + 1, d)
+        send_rest(g, (1,))
+        if more:
+            for copy in group_loads(g + 1, 1):
+                copy.wait()
+            look_values(g + 1, 0)
+        settle(g, 0, 1)
+        settle(g, 0, 0)
+    query_gradients(last)
+    for g in range(last):
+        finish(g, (1, 0))
+    finish(last, (1,))
+    send_rest(last, (0,))
+    finish(last, (0,))
 
     for g in range(kv_count):
         for t in range(2):
@@ -465,8 +501,8 @@
             pltpu.VMEM((kv_count, pairs, halves, width, 2 * HALF), f32),
             pltpu.VMEM((kv_count, pairs, halves, width, 2 * HALF), f32),
             pltpu.VMEM((kv_count, reach + 1, 3, pairs * halves, 2 * HALF), f32),
-            pltpu.VMEM((reach + 1, pairs * halves, 2 * HALF), f32),
-            pltpu.VMEM((pairs * halves, 2 * HALF), f32),
+            pltpu.VMEM((kv_count, reach + 1, pairs * halves, 2 * HALF), f32),
+            pltpu.VMEM((kv_count, pairs * halves, 2 * HALF), f32),
             pltpu.VMEM((halves, width, pairs * 2 * HALF), bf16),
             pltpu.VMEM((halves, width, pairs * 2 * HALF), bf16),
             pltpu.VMEM((2, kv_count, window, HEAD_SIZE), bf16),

time: 31.9 us -> 33.4 us (1.047)
  Pallas kernels: 31.1 us -> 32.6 us
    pallas_call x1, Pallas kernels: 29.9 us -> 31.4 us  [shards(): pl.pallas_call(functools.partial(kernel, n, reach, rows, per_kv, kv_count...]
where the time goes in v2:
time: 33.4 us; the launch traced here: 33.2 us
  Pallas kernels  32.6 us (98%)
  between operations  0.64 us (2%)
    pallas_call x1, Pallas kernels, shards(): pl.pallas_call(functools.partial(kernel, n, reach, rows, per_kv, kv_count...  31.4 us
    pallas_call x1, Pallas kernels, shards(): pl.pallas_call(functools.partial(place, kv_count, shared), out_shape=(jax...  1.2 us

profile of v2, /device:TPU:0, one launch (start us, length us, event | category | flops | bytes accessed | tf_op | source)
XLA Modules:
  0.0 33.2 jit_solution(2063117103305687239)
XLA Ops:
  0.6 31.4 %shard_map.76 = (bf16[256,2048]{1,0:T(8,128)(2,1)S(1)}, bf16[2,2,256,128]{3,2,1,0:T(8,128)(2,1)S(1)}, bf16[2,2,256,128]{3,2,1,0:T(8,128)(2,1)S(1)}) custom-call(bf16[256,2048]{1,0:T(8,128)(2,1)} %q_hbm.1, bf16[256,512]{1,0:T(8,128)(2,1)} %k_hbm.1, bf16[256,512]{1,0:T(8,128)(2,1)} %v_hbm.1, bf16[256,2048]{1,0:T(8,128)(2,1)} %g_hbm.1, s32[1,256]{1,0:T(1,128)} %bitcast.1), custom_call_target="tpu_custom_call" | custom-call | tf_op jit(solution)/shard_map/pallas_call | solution.py:489
  32.0 1.2 %shard_map.77 = (bf16[256,2048]{1,0:T(8,128)(2,1)}, bf16[256,512]{1,0:T(8,128)(2,1)}, bf16[256,512]{1,0:T(8,128)(2,1)}) custom-call(bf16[256,2048]{1,0:T(8,128)(2,1)S(1)} %get-tuple-element.6.dqv, bf16[2,2,256,128]{3,2,1,0:T(8,128)(2,1)S(1)} %get-tuple-element.7.fin, bf16[2,2,256,128]{3,2,1,0:T(8,128)(2,1)S(1)} %get-tuple-element.8.other), custom_call_target="tpu_custom_call" | custom-call | tf_op jit(solution)/shard_map/pallas_call | solution.py:532

commit v3 on v2

--- a/solution.py
+++ b/solution.py
@@ -21,9 +21,9 @@
     n, reach, rows, per_kv, kv_count, shared,
     q_hbm, k_hbm, v_hbm, g_hbm, seg_hbm,
     dqv, fin, other,
-    qv, gv, ev, dpv, stats, fac, deltas, pv, dsv, win, segwin, bias, kt, acc, sendb, ret, pfin,
+    qv, gv, ev, dpv, stats, fac, deltas, pv, dsv, win, segwin, bias, kt, acc, sendb, ret, far_ret, pfin,
     seg_sem, load_sem, own_sem, seg_send, seg_recv, send_sem, recv_sem, back_send, back_recv,
-    pair_send, pair_recv,
+    pair_send, pair_recv, far_back_send, far_back_recv,
 ):
     rank = lax.axis_index("ctx")
     kv = lax.axis_index("kv")
@@ -99,6 +99,24 @@
             device_id_type=MESH,
         )
 
+    def back_far(g, t, r):
+        return pltpu.make_async_remote_copy(
+            src_ref=sendb.at[g, 1, t, some(r)],
+            dst_ref=far_ret.at[g, t, some(r)],
+            send_sem=far_back_send.at[g, t, r],
+            recv_sem=far_back_recv.at[g, t, r],
+            device_id={"ctx": lax.rem(rank + n - 2, n)},
+            device_id_type=MESH,
+        )
+
+    far = reach > 1
+
+    def goes_far(of, g, t):
+        yes = of == 2
+        if g == kv_count - 1 and t in ():
+            yes = yes | (of == n - 1)
+        return yes
+
     def owed(g, d, t, r):
         return acc[g, t, pl.ds((reach - d) * rows + r * HALF, HALF), :]
 
@@ -132,12 +150,21 @@
         pl.semaphore_signal(barrier, inc=1, device_id={"ctx": down}, device_id_type=MESH)
 
     expected = 1 + jnp.where(has_up, 1, 0) + jnp.where(rank > 0, 1, 0)
+    if far:
+        @pl.when(rank == 0)
+        def _():
+            pl.semaphore_signal(
+                barrier, inc=1, device_id={"ctx": lax.rem(rank + 2, n)}, device_id_type=MESH
+            )
+
+        expected = expected + jnp.where(rank == 2, 1, 0)
     pl.semaphore_wait(barrier, expected)
 
     @pl.when(has_up)
     def _():
         forward_seg(0).start()
         forward(0, 0, 0).start()
+        forward(1, 0, 0).start()
 
     units = pairs * halves
 
@@ -282,7 +309,7 @@
                         pn = ev[g, p, h, at, :] * f
                         if t == 0:
                             delta = deltas[g, u:u + 1, :]
-                            dsv[h, at, there] = (
+                            dsv[g, h, at, there] = (
                                 pn * (dpv[g, p, h, at, :] - delta)
                             ).astype(jnp.bfloat16)
                         else:
@@ -290,7 +317,7 @@
             for i, h in enumerate(order):
                 lo, hi = part(d, h)
                 span = slice(lo + h * HALF, hi + h * HALF)
-                low, ref = ((dsv, qv), (pv, gv))[t]
+                low, ref = ((dsv.at[g], qv), (pv, gv))[t]
                 out = jnp.dot(
                     low[h, lo:hi, :], stack(ref, g, h), preferred_element_type=jnp.float32
                 )
@@ -306,30 +333,55 @@
                 kt[g, :, slot(d)] = win[0, g, slot(d), :].T
         for h in range(halves):
             dqt = jnp.dot(
-                kt[g, :, h * HALF:h * HALF + width], dsv[h], preferred_element_type=jnp.float32
+                kt[g, :, h * HALF:h * HALF + width], dsv[g, h], preferred_element_type=jnp.float32
             )
             dq = (dqt * scale).T.astype(jnp.bfloat16)
             for i in range(per_kv):
                 at = (g * per_kv + i) * HEAD_SIZE
                 dqv[h * HALF:(h + 1) * HALF, at:at + HEAD_SIZE] = dq[i * HALF:(i + 1) * HALF]
 
+    def start_back(g, d, t, r):
+        if far and d == 2:
+            away = goes_far(rank, g, t)
+
+            @pl.when(away)
+            def _():
+                back_far(g, t, r).start()
+
+            @pl.when(jnp.logical_not(away))
+            def _():
+                back(g, d, t, r).start()
+        else:
+            back(g, d, t, r).start()
+
+    def alone(g, d, t):
+        if d == reach:
+            return rank >= d
+        yes = jnp.logical_not(has_up)
+        if far and d == 1:
+            yes = yes | goes_far(rank + 1, g, t)
+        return (rank >= d) & yes
+
     def send_first(g, d, kinds):
-        @pl.when((rank >= d) if d == reach else ((rank >= d) & jnp.logical_not(has_up)))
-        def _():
-            for t, r in pieces(kinds):
-                sendb[g, d - 1, t, some(r), :] = owed(g, d, t, r).astype(jnp.bfloat16)
-                back(g, d, t, r).start()
+        for t in kinds:
+            @pl.when(alone(g, d, t))
+            def _(t=t):
+                for r in range(halves):
+                    sendb[g, d - 1, t, some(r), :] = owed(g, d, t, r).astype(jnp.bfloat16)
+                for r in range(halves):
+                    start_back(g, d, t, r)
 
     def send_rest(g, kinds):
         for d in range(reach - 1, 0, -1):
-            @pl.when(has_up & (rank >= d))
-            def _(d=d):
-                for t, r in pieces(kinds):
-                    back(g, d + 1, t, r).wait_recv()
-                    sendb[g, d - 1, t, some(r), :] = (
-                        owed(g, d, t, r) + ret[g, d, t, some(r), :].astype(jnp.float32)
-                    ).astype(jnp.bfloat16)
-                    back(g, d, t, r).start()
+            for t in kinds:
+                @pl.when((rank >= d) & jnp.logical_not(alone(g, d, t)))
+                def _(d=d, t=t):
+                    for r in range(halves):
+                        back(g, d + 1, t, r).wait_recv()
+                        sendb[g, d - 1, t, some(r), :] = (
+                            owed(g, d, t, r) + ret[g, d, t, some(r), :].astype(jnp.float32)
+                        ).astype(jnp.bfloat16)
+                        start_back(g, d, t, r)
 
     def finish(g, kinds):
         for t, r in pieces(kinds):
@@ -339,6 +391,14 @@
                 acc[g, t, pl.ds(reach * rows + r * HALF, HALF), :] += (
                     ret[g, 0, t, some(r), :].astype(jnp.float32)
                 )
+
+            if far:
+                @pl.when(goes_far(rank + 2, g, t))
+                def _(t=t, r=r):
+                    back_far(g, t, r).wait_recv()
+                    acc[g, t, pl.ds(reach * rows + r * HALF, HALF), :] += (
+                        far_ret[g, t, some(r), :].astype(jnp.float32)
+                    )
 
             factor = scale if t == 0 else 1.0
             fin[g, t, some(r), :] = (owed(g, 0, t, r) * factor).astype(jnp.bfloat16)
@@ -354,68 +414,83 @@
                 stats[g, d, 2] = jnp.zeros((units, 2 * HALF), jnp.float32)
             for h in range(halves):
                 lo, hi = part(d, h)
-                dsv[h, lo:hi, :] = jnp.zeros((hi - lo, pairs * 2 * HALF), jnp.bfloat16)
+                for g in range(kv_count):
+                    dsv[g, h, lo:hi, :] = jnp.zeros(
+                        (hi - lo, pairs * 2 * HALF), jnp.bfloat16
+                    )
 
     last = kv_count - 1
+    def ready(g, t):
+        for copy in group_loads(g, t):
+            copy.wait()
+
     seg_load.wait()
     make_bias(0)
-    for copy in group_loads(0, 0):
-        copy.wait()
+    ready(0, 0)
     look_keys(0, 0)
     for d in range(1, reach):
         receive_seg(d)
     for d in range(1, reach):
         receive(0, d, 0)
-    send_own(0, 1)
-    for d in range(1, reach):
         biased(d)
         look_keys(0, d)
-    for copy in group_loads(0, 1):
-        copy.wait()
+    ready(0, 1)
     look_values(0, 0)
+    for d in range(1, reach):
+        receive(0, d, 1)
+    if last > 0:
+        for t in range(2):
+            send_own(1, t)
+    for d in range(1, reach):
+        look_values(0, d)
     receive_seg(reach)
     biased(reach)
     for g in range(kv_count):
         more = g < last
+        if more:
+            ready(g + 1, 0)
+            look_keys(g + 1, 0)
         receive(g, reach, 0)
         look_keys(g, reach)
         combine_keys(g)
-        for d in range(reach, 0, -1):
+        settle(g, reach, 1)
+        send_first(g, reach, (1,))
+        for d in range(reach - 1, 0, -1):
             settle(g, d, 1)
-            send_first(g, d, (1,))
-        for d in range(1, reach):
-            receive(g, d, 1)
-        if more:
-            send_own(g + 1, 0)
-        for d in range(1, reach):
-            look_values(g, d)
+            if more:
+                send_first(g, d, (1,))
         if g > 0:
-            send_rest(g - 1, (0,))
-            query_gradients(g - 1)
-        if more:
-            for copy in group_loads(g + 1, 0):
-                copy.wait()
-            look_keys(g + 1, 0)
+            send_rest(g - 1, (1,))
         receive(g, reach, 1)
         look_values(g, reach)
         combine_values(g)
-        for d in range(reach, 0, -1):
+        settle(g, reach, 0)
+        send_first(g, reach, (0,))
+        for d in range(reach - 1, 0, -1):
+            if not more:
+                send_first(g, d, (1,))
             settle(g, d, 0)
             send_first(g, d, (0,))
         if more:
             for d in range(1, reach):
                 receive(g + 1, d, 0)
-            send_own(g + 1, 1)
+                look_keys(g + 1, d)
+            ready(g + 1, 1)
+            look_values(g + 1, 0)
             for d in range(1, reach):
-                look_keys(g + 1, d)
-        send_rest(g, (1,))
-        if more:
-            for copy in group_loads(g + 1, 1):
-                copy.wait()
-            look_values(g + 1, 0)
+                receive(g + 1, d, 1)
+            if g + 2 < kv_count:
+                for t in range(2):
+                    send_own(g + 2, t)
+            for d in range(1, reach):
+                look_values(g + 1, d)
+        if g > 0:
+            send_rest(g - 1, (0,))
         settle(g, 0, 1)
         settle(g, 0, 0)
-    query_gradients(last)
+    for g in range(kv_count):
+        query_gradients(g)
+    send_rest(last, (1,))
     for g in range(last):
         finish(g, (1, 0))
     finish(last, (1,))
@@ -440,11 +515,23 @@
                 for t in range(2):
                     forward(t, g, d).wait_send()
     for d in range(1, reach + 1):
-        @pl.when(rank >= d)
-        def _(d=d):
-            for g in range(kv_count):
-                for t, r in pieces((0, 1)):
-                    back(g, d, t, r).wait_send()
+        for g in range(kv_count):
+            for t in range(2):
+                if far and d == 2:
+                    @pl.when(goes_far(rank, g, t))
+                    def _(g=g, t=t):
+                        for r in range(halves):
+                            back_far(g, t, r).wait_send()
+
+                    @pl.when((rank >= d) & jnp.logical_not(goes_far(rank, g, t)))
+                    def _(g=g, t=t, d=d):
+                        for r in range(halves):
+                            back(g, d, t, r).wait_send()
+                else:
+                    @pl.when(rank >= d)
+                    def _(g=g, t=t, d=d):
+                        for r in range(halves):
+                            back(g, d, t, r).wait_send()
 
 
 def place(kv_count, shared, dqv, fin, other, dq_hbm, dk_hbm, dv_hbm, sem):
@@ -504,7 +591,7 @@
             pltpu.VMEM((kv_count, reach + 1, pairs * halves, 2 * HALF), f32),
             pltpu.VMEM((kv_count, pairs * halves, 2 * HALF), f32),
             pltpu.VMEM((halves, width, pairs * 2 * HALF), bf16),
-            pltpu.VMEM((halves, width, pairs * 2 * HALF), bf16),
+            pltpu.VMEM((kv_count, halves, width, pairs * 2 * HALF), bf16),
             pltpu.VMEM((2, kv_count, window, HEAD_SIZE), bf16),
             pltpu.VMEM((reach + 1, 1, rows), jnp.int32),
             pltpu.VMEM((halves, width, HALF), f32),
@@ -512,6 +599,7 @@
             pltpu.VMEM((kv_count, 2, window, HEAD_SIZE), f32),
             pltpu.VMEM((kv_count, reach, 2, rows, HEAD_SIZE), bf16),
             pltpu.VMEM((kv_count, reach, 2, rows, HEAD_SIZE), bf16),
+            pltpu.VMEM((kv_count, 2, rows, HEAD_SIZE), bf16),
             pltpu.VMEM((kv_count, 2, rows, HEAD_SIZE), bf16),
             dma((1,)),
             dma((2, head_count)),
@@ -522,6 +610,8 @@
             dma((2, kv_count, reach + 1)),
             dma((kv_count, reach, 2, halves)),
             dma((kv_count, reach, 2, halves)),
+            dma((kv_count, 2, halves)),
+            dma((kv_count, 2, halves)),
             dma((kv_count, 2, halves)),
             dma((kv_count, 2, halves)),
         ],

time: 33.4 us -> 29.4 us (0.88)
  the two profiles are of different devices: /device:TPU:0 before, /device:TPU:11 now
where the time goes in v3:
time: 29.4 us; the launch traced here: 29.2 us
  Pallas kernels  28.6 us (97%)
  between operations  0.64 us (2%)
    pallas_call x1, Pallas kernels, shards(): pl.pallas_call(functools.partial(kernel, n, reach, rows, per_kv, kv_count...  27.4 us
    pallas_call x1, Pallas kernels, shards(): pl.pallas_call(functools.partial(place, kv_count, shared), out_shape=(jax...  1.2 us

profile of v3, /device:TPU:11, one launch (start us, length us, event | category | flops | bytes accessed | tf_op | source)
XLA Modules:
  0.0 29.2 jit_solution(12285315128605497613)
XLA Ops:
  0.6 27.4 %shard_map.76 = (bf16[256,2048]{1,0:T(8,128)(2,1)S(1)}, bf16[2,2,256,128]{3,2,1,0:T(8,128)(2,1)S(1)}, bf16[2,2,256,128]{3,2,1,0:T(8,128)(2,1)S(1)}) custom-call(bf16[256,2048]{1,0:T(8,128)(2,1)} %q_hbm.1, bf16[256,512]{1,0:T(8,128)(2,1)} %k_hbm.1, bf16[256,512]{1,0:T(8,128)(2,1)} %v_hbm.1, bf16[256,2048]{1,0:T(8,128)(2,1)} %g_hbm.1, s32[1,256]{1,0:T(1,128)} %bitcast.1), custom_call_target="tpu_custom_call" | custom-call | tf_op jit(solution)/shard_map/pallas_call | solution.py:576
  28.0 1.2 %shard_map.77 = (bf16[256,2048]{1,0:T(8,128)(2,1)}, bf16[256,512]{1,0:T(8,128)(2,1)}, bf16[256,512]{1,0:T(8,128)(2,1)}) custom-call(bf16[256,2048]{1,0:T(8,128)(2,1)S(1)} %get-tuple-element.6.dqv, bf16[2,2,256,128]{3,2,1,0:T(8,128)(2,1)S(1)} %get-tuple-element.7.fin, bf16[2,2,256,128]{3,2,1,0:T(8,128)(2,1)S(1)} %get-tuple-element.8.other), custom_call_target="tpu_custom_call" | custom-call | tf_op jit(solution)/shard_map/pallas_call | solution.py:622

commit v4 on v3

--- a/solution.py
+++ b/solution.py
@@ -61,14 +61,18 @@
     def group_loads(g, t):
         return [own(t, g)] + [load(t, i) for i in range(g * per_kv, (g + 1) * per_kv)]
 
-    def forward(t, g, d):
+    def some(r):
+        return pl.ds(r * HALF, HALF)
+
+    def forward(t, g, d, r):
         ref = k_hbm if t == 0 else v_hbm
-        src = ref.at[:, cols(first, g)] if d == 0 else win.at[t, g, slot(d)]
+        at = (reach - d) * rows + r * HALF
+        src = ref.at[some(r), cols(first, g)] if d == 0 else win.at[t, g, pl.ds(at, HALF)]
         return pltpu.make_async_remote_copy(
             src_ref=src,
-            dst_ref=win.at[t, g, slot(d + 1)],
-            send_sem=send_sem.at[t, g, d],
-            recv_sem=recv_sem.at[t, g, d + 1],
+            dst_ref=win.at[t, g, pl.ds(at - rows, HALF)],
+            send_sem=send_sem.at[t, g, d, r],
+            recv_sem=recv_sem.at[t, g, d + 1, r],
             device_id={"ctx": up},
             device_id_type=MESH,
         )
@@ -86,9 +90,6 @@
     def pieces(kinds):
         return [(t, r) for t in kinds for r in range(halves)]
 
-    def some(r):
-        return pl.ds(r * HALF, HALF)
-
     def back(g, d, t, r):
         return pltpu.make_async_remote_copy(
             src_ref=sendb.at[g, d - 1, t, some(r)],
@@ -132,12 +133,6 @@
 
     has_up = rank < n - 1
 
-    seg_load.start()
-    for g in range(kv_count):
-        for t in range(2):
-            for copy in group_loads(g, t):
-                copy.start()
-
     barrier = pltpu.get_barrier_semaphore()
     pl.semaphore_signal(barrier, inc=1, device_id={"kv": mate}, device_id_type=MESH)
 
@@ -158,13 +153,20 @@
             )
 
         expected = expected + jnp.where(rank == 2, 1, 0)
+    seg_load.start()
+    for g in range(kv_count):
+        for t in range(2):
+            for copy in group_loads(g, t):
+                copy.start()
+
     pl.semaphore_wait(barrier, expected)
 
     @pl.when(has_up)
     def _():
         forward_seg(0).start()
-        forward(0, 0, 0).start()
-        forward(1, 0, 0).start()
+        for t in range(2):
+            for r in range(halves):
+                forward(t, 0, 0, r).start()
 
     units = pairs * halves
 
@@ -179,19 +181,21 @@
                 forward_seg(d).start()
 
     def receive(g, d, t):
-        @pl.when(rank >= d)
-        def _():
-            forward(t, g, d - 1).wait_recv()
-
-        if d < reach:
-            @pl.when((rank >= d) & has_up)
-            def _():
-                forward(t, g, d).start()
+        for r in range(halves):
+            @pl.when(rank >= d)
+            def _(r=r):
+                forward(t, g, d - 1, r).wait_recv()
+
+            if d < reach:
+                @pl.when((rank >= d) & has_up)
+                def _(r=r):
+                    forward(t, g, d, r).start()
 
     def send_own(g, t):
         @pl.when(has_up)
         def _():
-            forward(t, g, 0).start()
+            for r in range(halves):
+                forward(t, g, 0, r).start()
 
     def part(d, h):
         start = (reach - d) * rows - h * HALF
@@ -450,6 +454,8 @@
         if more:
             ready(g + 1, 0)
             look_keys(g + 1, 0)
+        if g > 0:
+            send_rest(g - 1, (1,))
         receive(g, reach, 0)
         look_keys(g, reach)
         combine_keys(g)
@@ -460,7 +466,7 @@
             if more:
                 send_first(g, d, (1,))
         if g > 0:
-            send_rest(g - 1, (1,))
+            send_rest(g - 1, (0,))
         receive(g, reach, 1)
         look_values(g, reach)
         combine_values(g)
@@ -484,17 +490,15 @@
                     send_own(g + 2, t)
             for d in range(1, reach):
                 look_values(g + 1, d)
-        if g > 0:
-            send_rest(g - 1, (0,))
         settle(g, 0, 1)
         settle(g, 0, 0)
     for g in range(kv_count):
         query_gradients(g)
     send_rest(last, (1,))
+    send_rest(last, (0,))
     for g in range(last):
         finish(g, (1, 0))
     finish(last, (1,))
-    send_rest(last, (0,))
     finish(last, (0,))
 
     for g in range(kv_count):
@@ -513,7 +517,8 @@
             forward_seg(d).wait_send()
             for g in range(kv_count):
                 for t in range(2):
-                    forward(t, g, d).wait_send()
+                    for r in range(halves):
+                        forward(t, g, d, r).wait_send()
     for d in range(1, reach + 1):
         for g in range(kv_count):
             for t in range(2):
@@ -606,8 +611,8 @@
             dma((2, kv_count)),
             dma((reach + 1,)),
             dma((reach + 1,)),
-            dma((2, kv_count, reach + 1)),
-            dma((2, kv_count, reach + 1)),
+            dma((2, kv_count, reach + 1, halves)),
+            dma((2, kv_count, reach + 1, halves)),
             dma((kv_count, reach, 2, halves)),
             dma((kv_count, reach, 2, halves)),
             dma((kv_count, 2, halves)),

time: 29.4 us -> 28.1 us (0.956)
  the two profiles are of different devices: /device:TPU:11 before, /device:TPU:0 now
where the time goes in v4:
time: 28.1 us; the launch traced here: 27.7 us
  Pallas kernels  27.1 us (96%)
  between operations  0.64 us (2%)
    pallas_call x1, Pallas kernels, shards(): pl.pallas_call(functools.partial(kernel, n, reach, rows, per_kv, kv_count...  25.9 us
    pallas_call x1, Pallas kernels, shards(): pl.pallas_call(functools.partial(place, kv_count, shared), out_shape=(jax...  1.2 us

profile of v4, /device:TPU:0, one launch (start us, length us, event | category | flops | bytes accessed | tf_op | source)
XLA Modules:
  0.0 27.7 jit_solution(17028770570197548361)
XLA Ops:
  0.6 25.9 %shard_map.76 = (bf16[256,2048]{1,0:T(8,128)(2,1)S(1)}, bf16[2,2,256,128]{3,2,1,0:T(8,128)(2,1)S(1)}, bf16[2,2,256,128]{3,2,1,0:T(8,128)(2,1)S(1)}) custom-call(bf16[256,2048]{1,0:T(8,128)(2,1)} %q_hbm.1, bf16[256,512]{1,0:T(8,128)(2,1)} %k_hbm.1, bf16[256,512]{1,0:T(8,128)(2,1)} %v_hbm.1, bf16[256,2048]{1,0:T(8,128)(2,1)} %g_hbm.1, s32[1,256]{1,0:T(1,128)} %bitcast.1), custom_call_target="tpu_custom_call" | custom-call | tf_op jit(solution)/shard_map/pallas_call | solution.py:581
  26.5 1.2 %shard_map.77 = (bf16[256,2048]{1,0:T(8,128)(2,1)}, bf16[256,512]{1,0:T(8,128)(2,1)}, bf16[256,512]{1,0:T(8,128)(2,1)}) custom-call(bf16[256,2048]{1,0:T(8,128)(2,1)S(1)} %get-tuple-element.6.dqv, bf16[2,2,256,128]{3,2,1,0:T(8,128)(2,1)S(1)} %get-tuple-element.7.fin, bf16[2,2,256,128]{3,2,1,0:T(8,128)(2,1)S(1)} %get-tuple-element.8.other), custom_call_target="tpu_custom_call" | custom-call | tf_op jit(solution)/shard_map/pallas_call | solution.py:627

commit v5 on v4

--- a/solution.py
+++ b/solution.py
@@ -11,6 +11,7 @@
 HEAD_SIZE = 128
 HALF = 128
 CHUNK = 32
+PIECE = 128
 LOG2E = 1.4426950408889634
 NEG = -1e30
 MESH = pl.DeviceIdType.MESH
@@ -87,13 +88,18 @@
             device_id_type=MESH,
         )
 
+    bits = rows // PIECE
+
+    def bit(r):
+        return pl.ds(r * PIECE, PIECE)
+
     def pieces(kinds):
-        return [(t, r) for t in kinds for r in range(halves)]
+        return [(t, r) for t in kinds for r in range(bits)]
 
     def back(g, d, t, r):
         return pltpu.make_async_remote_copy(
-            src_ref=sendb.at[g, d - 1, t, some(r)],
-            dst_ref=ret.at[g, d - 1, t, some(r)],
+            src_ref=sendb.at[g, d - 1, t, bit(r)],
+            dst_ref=ret.at[g, d - 1, t, bit(r)],
             send_sem=back_send.at[g, d - 1, t, r],
             recv_sem=back_recv.at[g, d - 1, t, r],
             device_id={"ctx": down},
@@ -102,8 +108,8 @@
 
     def back_far(g, t, r):
         return pltpu.make_async_remote_copy(
-            src_ref=sendb.at[g, 1, t, some(r)],
-            dst_ref=far_ret.at[g, t, some(r)],
+            src_ref=sendb.at[g, 1, t, bit(r)],
+            dst_ref=far_ret.at[g, t, bit(r)],
             send_sem=far_back_send.at[g, t, r],
             recv_sem=far_back_recv.at[g, t, r],
             device_id={"ctx": lax.rem(rank + n - 2, n)},
@@ -119,12 +125,12 @@
         return yes
 
     def owed(g, d, t, r):
-        return acc[g, t, pl.ds((reach - d) * rows + r * HALF, HALF), :]
+        return acc[g, t, pl.ds((reach - d) * rows + r * PIECE, PIECE), :]
 
     def to_mate(g, t, r):
         return pltpu.make_async_remote_copy(
-            src_ref=fin.at[g, t, some(r)],
-            dst_ref=pfin.at[g, t, some(r)],
+            src_ref=fin.at[g, t, bit(r)],
+            dst_ref=pfin.at[g, t, bit(r)],
             send_sem=pair_send.at[g, t, r],
             recv_sem=pair_recv.at[g, t, r],
             device_id={"kv": mate},
@@ -370,9 +376,9 @@
         for t in kinds:
             @pl.when(alone(g, d, t))
             def _(t=t):
-                for r in range(halves):
-                    sendb[g, d - 1, t, some(r), :] = owed(g, d, t, r).astype(jnp.bfloat16)
-                for r in range(halves):
+                for r in range(bits):
+                    sendb[g, d - 1, t, bit(r), :] = owed(g, d, t, r).astype(jnp.bfloat16)
+                for r in range(bits):
                     start_back(g, d, t, r)
 
     def send_rest(g, kinds):
@@ -380,10 +386,10 @@
             for t in kinds:
                 @pl.when((rank >= d) & jnp.logical_not(alone(g, d, t)))
                 def _(d=d, t=t):
-                    for r in range(halves):
+                    for r in range(bits):
                         back(g, d + 1, t, r).wait_recv()
-                        sendb[g, d - 1, t, some(r), :] = (
-                            owed(g, d, t, r) + ret[g, d, t, some(r), :].astype(jnp.float32)
+                        sendb[g, d - 1, t, bit(r), :] = (
+                            owed(g, d, t, r) + ret[g, d, t, bit(r), :].astype(jnp.float32)
                         ).astype(jnp.bfloat16)
                         start_back(g, d, t, r)
 
@@ -392,20 +398,20 @@
             @pl.when(has_up)
             def _(t=t, r=r):
                 back(g, 1, t, r).wait_recv()
-                acc[g, t, pl.ds(reach * rows + r * HALF, HALF), :] += (
-                    ret[g, 0, t, some(r), :].astype(jnp.float32)
+                acc[g, t, pl.ds(reach * rows + r * PIECE, PIECE), :] += (
+                    ret[g, 0, t, bit(r), :].astype(jnp.float32)
                 )
 
             if far:
                 @pl.when(goes_far(rank + 2, g, t))
                 def _(t=t, r=r):
                     back_far(g, t, r).wait_recv()
-                    acc[g, t, pl.ds(reach * rows + r * HALF, HALF), :] += (
-                        far_ret[g, t, some(r), :].astype(jnp.float32)
+                    acc[g, t, pl.ds(reach * rows + r * PIECE, PIECE), :] += (
+                        far_ret[g, t, bit(r), :].astype(jnp.float32)
                     )
 
             factor = scale if t == 0 else 1.0
-            fin[g, t, some(r), :] = (owed(g, 0, t, r) * factor).astype(jnp.bfloat16)
+            fin[g, t, bit(r), :] = (owed(g, 0, t, r) * factor).astype(jnp.bfloat16)
             to_mate(g, t, r).start()
 
     for d in range(1, reach + 1):
@@ -461,9 +467,9 @@
         combine_keys(g)
         settle(g, reach, 1)
         send_first(g, reach, (1,))
-        for d in range(reach - 1, 0, -1):
-            settle(g, d, 1)
-            if more:
+        if more:
+            for d in range(reach - 1, 0, -1):
+                settle(g, d, 1)
                 send_first(g, d, (1,))
         if g > 0:
             send_rest(g - 1, (0,))
@@ -474,6 +480,7 @@
         send_first(g, reach, (0,))
         for d in range(reach - 1, 0, -1):
             if not more:
+                settle(g, d, 1)
                 send_first(g, d, (1,))
             settle(g, d, 0)
             send_first(g, d, (0,))
@@ -490,27 +497,15 @@
                     send_own(g + 2, t)
             for d in range(1, reach):
                 look_values(g + 1, d)
+    for g in range(last):
         settle(g, 0, 1)
         settle(g, 0, 0)
-    for g in range(kv_count):
         query_gradients(g)
     send_rest(last, (1,))
+    settle(last, 0, 1)
+    settle(last, 0, 0)
     send_rest(last, (0,))
-    for g in range(last):
-        finish(g, (1, 0))
-    finish(last, (1,))
-    finish(last, (0,))
-
-    for g in range(kv_count):
-        for t in range(2):
-            for r in range(halves):
-                to_mate(g, t, r).wait()
-            if shared:
-                other[g, t] = (
-                    fin[g, t].astype(jnp.float32) + pfin[g, t].astype(jnp.float32)
-                ).astype(jnp.bfloat16)
-            else:
-                other[g, t] = pfin[g, t]
+    query_gradients(last)
     for d in range(reach):
         @pl.when(has_up & (rank >= d))
         def _(d=d):
@@ -519,23 +514,38 @@
                 for t in range(2):
                     for r in range(halves):
                         forward(t, g, d, r).wait_send()
+    for g in range(last):
+        finish(g, (1, 0))
+    finish(last, (1,))
+    finish(last, (0,))
+
+    for g in range(kv_count):
+        for t in range(2):
+            for r in range(bits):
+                to_mate(g, t, r).wait()
+            if shared:
+                other[g, t] = (
+                    fin[g, t].astype(jnp.float32) + pfin[g, t].astype(jnp.float32)
+                ).astype(jnp.bfloat16)
+            else:
+                other[g, t] = pfin[g, t]
     for d in range(1, reach + 1):
         for g in range(kv_count):
             for t in range(2):
                 if far and d == 2:
                     @pl.when(goes_far(rank, g, t))
                     def _(g=g, t=t):
-                        for r in range(halves):
+                        for r in range(bits):
                             back_far(g, t, r).wait_send()
 
                     @pl.when((rank >= d) & jnp.logical_not(goes_far(rank, g, t)))
                     def _(g=g, t=t, d=d):
-                        for r in range(halves):
+                        for r in range(bits):
                             back(g, d, t, r).wait_send()
                 else:
                     @pl.when(rank >= d)
                     def _(g=g, t=t, d=d):
-                        for r in range(halves):
+                        for r in range(bits):
                             back(g, d, t, r).wait_send()
 
 
@@ -613,12 +623,12 @@
             dma((reach + 1,)),
             dma((2, kv_count, reach + 1, halves)),
             dma((2, kv_count, reach + 1, halves)),
-            dma((kv_count, reach, 2, halves)),
-            dma((kv_count, reach, 2, halves)),
-            dma((kv_count, 2, halves)),
-            dma((kv_count, 2, halves)),
-            dma((kv_count, 2, halves)),
-            dma((kv_count, 2, halves)),
+            dma((kv_count, reach, 2, rows // PIECE)),
+            dma((kv_count, reach, 2, rows // PIECE)),
+            dma((kv_count, 2, rows // PIECE)),
+            dma((kv_count, 2, rows // PIECE)),
+            dma((kv_count, 2, rows // PIECE)),
+            dma((kv_count, 2, rows // PIECE)),
         ],
         compiler_params=pltpu.CompilerParams(
             collective_id=0, has_side_effects=True, vmem_limit_bytes=56 * 1024 * 1024

time: 28.1 us -> 27.9 us (level)
  no operation moved by 1% of the time
where the time goes in v5:
time: 27.9 us; the launch traced here: 27.5 us
  Pallas kernels  26.9 us (96%)
  between operations  0.64 us (2%)
    pallas_call x1, Pallas kernels, shards(): pl.pallas_call(functools.partial(kernel, n, reach, rows, per_kv, kv_count...  25.7 us
    pallas_call x1, Pallas kernels, shards(): pl.pallas_call(functools.partial(place, kv_count, shared), out_shape=(jax...  1.2 us

profile of v5, /device:TPU:0, one launch (start us, length us, event | category | flops | bytes accessed | tf_op | source)
XLA Modules:
  0.0 27.5 jit_solution(3811619156765142548)
XLA Ops:
  0.6 25.7 %shard_map.76 = (bf16[256,2048]{1,0:T(8,128)(2,1)S(1)}, bf16[2,2,256,128]{3,2,1,0:T(8,128)(2,1)S(1)}, bf16[2,2,256,128]{3,2,1,0:T(8,128)(2,1)S(1)}) custom-call(bf16[256,2048]{1,0:T(8,128)(2,1)} %q_hbm.1, bf16[256,512]{1,0:T(8,128)(2,1)} %k_hbm.1, bf16[256,512]{1,0:T(8,128)(2,1)} %v_hbm.1, bf16[256,2048]{1,0:T(8,128)(2,1)} %g_hbm.1, s32[1,256]{1,0:T(1,128)} %bitcast.1), custom_call_target="tpu_custom_call" | custom-call | tf_op jit(solution)/shard_map/pallas_call | solution.py:591
  26.3 1.2 %shard_map.77 = (bf16[256,2048]{1,0:T(8,128)(2,1)}, bf16[256,512]{1,0:T(8,128)(2,1)}, bf16[256,512]{1,0:T(8,128)(2,1)}) custom-call(bf16[256,2048]{1,0:T(8,128)(2,1)S(1)} %get-tuple-element.6.dqv, bf16[2,2,256,128]{3,2,1,0:T(8,128)(2,1)S(1)} %get-tuple-element.7.fin, bf16[2,2,256,128]{3,2,1,0:T(8,128)(2,1)S(1)} %get-tuple-element.8.other), custom_call_target="tpu_custom_call" | custom-call | tf_op jit(solution)/shard_map/pallas_call | solution.py:637

commit v6 on v5

--- a/solution.py
+++ b/solution.py
@@ -471,13 +471,13 @@
             for d in range(reach - 1, 0, -1):
                 settle(g, d, 1)
                 send_first(g, d, (1,))
-        if g > 0:
-            send_rest(g - 1, (0,))
         receive(g, reach, 1)
         look_values(g, reach)
         combine_values(g)
         settle(g, reach, 0)
         send_first(g, reach, (0,))
+        if g > 0:
+            send_rest(g - 1, (0,))
         for d in range(reach - 1, 0, -1):
             if not more:
                 settle(g, d, 1)

time: 27.9 us -> 27.9 us (level)
  the two profiles are of different devices: /device:TPU:0 before, /device:TPU:9 now
where the time goes in v6:
time: 27.9 us; the launch traced here: 27.8 us
  Pallas kernels  27.1 us (97%)
  between operations  0.64 us (2%)
    pallas_call x1, Pallas kernels, shards(): pl.pallas_call(functools.partial(kernel, n, reach, rows, per_kv, kv_count...  25.9 us
    pallas_call x1, Pallas kernels, shards(): pl.pallas_call(functools.partial(place, kv_count, shared), out_shape=(jax...  1.2 us

profile of v6, /device:TPU:9, one launch (start us, length us, event | category | flops | bytes accessed | tf_op | source)
XLA Modules:
  0.0 27.8 jit_solution(16380873532956137292)
XLA Ops:
  0.6 25.9 %shard_map.76 = (bf16[256,2048]{1,0:T(8,128)(2,1)S(1)}, bf16[2,2,256,128]{3,2,1,0:T(8,128)(2,1)S(1)}, bf16[2,2,256,128]{3,2,1,0:T(8,128)(2,1)S(1)}) custom-call(bf16[256,2048]{1,0:T(8,128)(2,1)} %q_hbm.1, bf16[256,512]{1,0:T(8,128)(2,1)} %k_hbm.1, bf16[256,512]{1,0:T(8,128)(2,1)} %v_hbm.1, bf16[256,2048]{1,0:T(8,128)(2,1)} %g_hbm.1, s32[1,256]{1,0:T(1,128)} %bitcast.1), custom_call_target="tpu_custom_call" | custom-call | tf_op jit(solution)/shard_map/pallas_call | solution.py:591
  26.6 1.2 %shard_map.77 = (bf16[256,2048]{1,0:T(8,128)(2,1)}, bf16[256,512]{1,0:T(8,128)(2,1)}, bf16[256,512]{1,0:T(8,128)(2,1)}) custom-call(bf16[256,2048]{1,0:T(8,128)(2,1)S(1)} %get-tuple-element.6.dqv, bf16[2,2,256,128]{3,2,1,0:T(8,128)(2,1)S(1)} %get-tuple-element.7.fin, bf16[2,2,256,128]{3,2,1,0:T(8,128)(2,1)S(1)} %get-tuple-element.8.other), custom_call_target="tpu_custom_call" | custom-call | tf_op jit(solution)/shard_map/pallas_call | solution.py:637
